TPU v7x, 128 devices: a whole 4x4x4 slice. The times are simulated.
128 devices in a mesh: row: 16 (over z, y), proto: 8 (over x, core).
Axes of the slice: x: 4, y: 4, z: 4, core: 2. Of those that a mesh axis runs over, the one named last changes fastest.
Arguments:
- embeddings: bfloat16 [4096, 256], P('row')
- queue_feats: bfloat16 [8192, 256], P('row')
- prototypes: bfloat16 [256, 65536], P('row', 'proto')
- crop_image: int32 [4096], P('row'), may hold values from 0 to 511, as said below
- fill_count: int32 [1], replicated, may hold values from 4096 to 8192
Outputs:
- grad_embed: float32 [4096, 256], P('row')
- grad_proto: float32 [256, 65536], P('row', 'proto')
- loss: float32 [1], replicated
Inputs may be any that keep to these rules, and one draw needn't show every extreme that they name: `crop_image`: each image index is named by exactly 8 crops, all within one aligned block of 256 rows (the rows of one device); block b holds images b * 32 to (b + 1) * 32 - 1.
All inputs are finite; a program needn't handle non-finite values.
Results may differ from a plain program's by a relative error of at most 0.002.
Values may be sent and summed in bfloat16 or wider, within the bound.
A program may use at most 64 MiB of HBM per device.

v0:
```python
import jax
import jax.numpy as jnp
from jax import lax
from jax.sharding import PartitionSpec as P

CROPS = 8
ITERS = 3
ENTROPY_SMOOTHER = 0.05
SOFTMAX_TEMPER = 0.1


def unit_rows(raw):
    values = raw.astype(jnp.float32)
    inverse = lax.rsqrt(jnp.sum(values * values, axis=1, keepdims=True) + 1e-06)
    return (values * inverse, inverse)


def body(embeddings, queue_feats, prototypes, crop_image, fill_count):
    normed_exact, inverse = unit_rows(embeddings)
    normed = normed_exact.astype(jnp.bfloat16)
    queue_normed = unit_rows(queue_feats)[0].astype(jnp.bfloat16)
    batch_rows = normed.shape[0]
    queue_rows = queue_normed.shape[0]
    feat_dim = normed.shape[1]
    image_local = batch_rows // CROPS
    local_image = crop_image - lax.axis_index("row") * image_local
    image_ids = jnp.arange(image_local, dtype=jnp.int32)
    membership = (image_ids[:, None] == local_image[None, :]).astype(jnp.bfloat16)
    gathered = lax.all_gather(prototypes, "row", axis=0, tiled=True)
    width_local = gathered.shape[1]
    block_cols = min(512, width_local)
    block_count = width_local // block_cols
    blocks = gathered.reshape(feat_dim, block_count, block_cols).transpose(1, 0, 2)
    offset = lax.axis_index("row") * queue_rows
    queue_live = (offset + jnp.arange(queue_rows, dtype=jnp.int32) < fill_count[0]).astype(
        jnp.float32
    )
    live = jnp.concatenate([jnp.ones((batch_rows,), jnp.float32), queue_live])
    rows_all = jnp.concatenate([normed, queue_normed], axis=0)

    def row_pass(column):

        def row_block(cumulative_accumulator, inputs_pair):
            proto_block, cluster_rescaling = inputs_pair
            centroid_similarity = jnp.dot(rows_all, proto_block, preferred_element_type=jnp.float32)
            return (
                cumulative_accumulator
                + jnp.sum(
                    jnp.exp(centroid_similarity / ENTROPY_SMOOTHER) * cluster_rescaling[None, :],
                    axis=1,
                ),
                None,
            )

        row_total, _ = lax.scan(
            row_block,
            jnp.zeros((rows_all.shape[0],), jnp.float32),
            (blocks, column.reshape(block_count, block_cols)),
        )
        return row_total

    centroid_matrix = live
    column = jnp.zeros((width_local,), jnp.float32)
    for sweep_index in range(ITERS):

        def column_block(proto_block):
            centroid_similarity = jnp.dot(rows_all, proto_block, preferred_element_type=jnp.float32)
            return jnp.sum(
                jnp.exp(centroid_similarity / ENTROPY_SMOOTHER) * centroid_matrix[:, None], axis=0
            )

        column = 1.0 / lax.psum(lax.map(column_block, blocks).reshape(width_local), "row")
        if sweep_index + 1 < ITERS:
            centroid_matrix = live / lax.psum(row_pass(column), "proto")
    column_blocks = column.reshape(block_count, block_cols)

    def totals(cumulative_accumulator, inputs_pair):
        proto_block, cluster_rescaling = inputs_pair
        centroid_similarity = jnp.dot(normed, proto_block, preferred_element_type=jnp.float32)
        allotment_share = jnp.sum(
            jnp.exp(centroid_similarity / ENTROPY_SMOOTHER) * cluster_rescaling[None, :], axis=1
        )
        softmax_portion = jnp.sum(jnp.exp(centroid_similarity / SOFTMAX_TEMPER), axis=1)
        return (
            (
                cumulative_accumulator[0] + allotment_share,
                cumulative_accumulator[1] + softmax_portion,
            ),
            None,
        )

    zeros_batch = jnp.zeros((batch_rows,), jnp.float32)
    (code_local, soft_local), _ = lax.scan(
        totals, (zeros_batch, zeros_batch), (blocks, column_blocks)
    )
    overall_mass_sum, softmax_total = lax.psum((code_local, soft_local), "proto")
    log_grand_total = jnp.log(softmax_total)
    member_weights = membership.astype(jnp.float32)

    def slopes(cumulative_accumulator, inputs_pair):
        proto_block, cluster_rescaling = inputs_pair
        centroid_similarity = jnp.dot(normed, proto_block, preferred_element_type=jnp.float32)
        cluster_allotment = (
            jnp.exp(centroid_similarity / ENTROPY_SMOOTHER)
            * cluster_rescaling[None, :]
            / overall_mass_sum[:, None]
        )
        per_image = jnp.dot(member_weights, cluster_allotment, precision=lax.Precision.HIGHEST)
        grouped = lax.dot_general(
            member_weights, per_image, (((0,), (0,)), ((), ())), precision=lax.Precision.HIGHEST
        )
        target_codes = (grouped - cluster_allotment) / (CROPS - 1)
        predicted_probs = jnp.exp(centroid_similarity / SOFTMAX_TEMPER) / softmax_total[:, None]
        logit_gradient = ((predicted_probs - target_codes) / SOFTMAX_TEMPER).astype(jnp.bfloat16)
        loss_portion = jnp.sum(
            target_codes * (log_grand_total[:, None] - centroid_similarity / SOFTMAX_TEMPER)
        )
        return (cumulative_accumulator + loss_portion, logit_gradient)

    loss_local, grad_blocks = lax.scan(slopes, jnp.zeros((), jnp.float32), (blocks, column_blocks))
    logit_gradient = grad_blocks.transpose(1, 0, 2).reshape(batch_rows, width_local)
    normed_local = lax.dot_general(
        logit_gradient, gathered, (((1,), (1,)), ((), ())), preferred_element_type=jnp.float32
    )
    normed_grad = lax.psum(normed_local, "proto")
    grad_proto = lax.psum_scatter(
        lax.dot_general(
            normed, logit_gradient, (((0,), (0,)), ((), ())), preferred_element_type=jnp.float32
        ),
        "row",
        scatter_dimension=0,
        tiled=True,
    )
    loss_total = lax.psum(loss_local, ("row", "proto"))
    loss = loss_total / (batch_rows * lax.axis_size("row"))
    grad_embed = inverse * (
        normed_grad - normed_exact * jnp.sum(normed_exact * normed_grad, axis=1, keepdims=True)
    )
    return (grad_embed, grad_proto, loss.reshape(1))


def solution(mesh):
    placed = (P("row", None), P("row", None), P("row", "proto"), P("row"), P())
    return jax.shard_map(
        body,
        mesh=mesh,
        in_specs=placed,
        out_specs=(P("row", None), P("row", "proto"), P()),
        check_vma=False,
    )
```

profile of v0, /device:TPU:0, one launch (start us, length us, event | category | flops | bytes accessed | tf_op | source)
XLA Modules:
  0.0 706.2 jit_solution(11963652205974593261)
XLA Ops:
  13.7 50.5 %all-gather.2.cloned.1.call-done = bf16[256,8192]{1,0:T(8,128)(2,1)} async-done(((bf16[16,8192]{1,0:T(8,128)(2,1)}), bf16[256,8192]{1,0:T(8,128)(2,1)}) %all-gather.2.cloned.1.call-update) | async-done | bytes 4194320 | tf_op jit(solution)/shard_map/all_gather | solution.py:29
  64.2 6.4 copy.16
  70.5 6.4 copy.23
  77.0 25.4 %while.78 = (s32[]{:T(128)}, f32[16,512]{1,0:T(8,128)S(1)}, bf16[16,256,512]{2,1,0:T(8,128)(2,1)}, bf16[768,256]{1,0:T(8,128)(2,1)S(1)}, f32[768]{0:T(1024)S(1)}, /*index=5*/s32[]{:T(128)}, s32[]{:T(128)}) while((s32[]{:T(128)}, f32[16,512]{1,0:T(8,128)S(1)}, bf16[16,256,512]{2,1,0:T(8,128)(2,1)}, bf16[768,256]{1,0:T(8,128)(2,1)S(1)}, ...), condition=%wide.region_4.5_spmd, body=%wide.region_2.4_spmd.sunk | while | flops 202505728 | bytes 664669 | solution.py:72
  81.7 1.5 multiply_reduce_fusion.13
  86.5 1.5 multiply_reduce_fusion.13
  91.3 1.5 multiply_reduce_fusion.13
  96.1 1.5 multiply_reduce_fusion.13
  100.8 1.5 multiply_reduce_fusion.13
  102.4 72.4 %psum.63 = f32[8192]{0:T(1024)S(1)} all-reduce(f32[8192]{0:T(1024)S(1)} %bitcast.113), channel_id=1, replica_groups=mesh['row'=16,'proto'=8] {'row'}, use_global_device_ids=true, to_apply=%region_5.6 | all-reduce | flops 8192 | bytes 65536 | tf_op jit(solution)/shard_map/psum | solution.py:72
  174.9 24.7 %while.82 = (s32[]{:T(128)}, f32[768]{0:T(1024)S(1)}, bf16[16,256,512]{2,1,0:T(8,128)(2,1)}, bf16[768,256]{1,0:T(8,128)(2,1)S(1)}, f32[16,512]{1,0:T(8,128)S(1)}, /*index=5*/s32[]{:T(128)}, s32[]{:T(128)}) while((s32[]{:T(128)}, f32[768]{0:T(1024)S(1)}, bf16[16,256,512]{2,1,0:T(8,128)(2,1)}, bf16[768,256]{1,0:T(8,128)(2,1)S(1)}, ...), condition=%wide.region_8.9_spmd.clone, body=%wide.region_6.8_spmd.clone.sunk | while | flops 202507008 | bytes 673895 | solution.py:55
  199.6 12.4 %psum.64 = f32[768]{0:T(1024)S(1)} all-reduce(f32[768]{0:T(1024)S(1)} %get-tuple-element.225), channel_id=1, replica_groups=mesh['row'=16,'proto'=8] {'proto'}, use_global_device_ids=true, to_apply=%region_9.10 | all-reduce | flops 768 | bytes 6144 | tf_op jit(solution)/shard_map/psum | solution.py:74
  212.0 25.5 %while.79 = (s32[]{:T(128)}, f32[16,512]{1,0:T(8,128)S(1)}, bf16[16,256,512]{2,1,0:T(8,128)(2,1)}, bf16[768,256]{1,0:T(8,128)(2,1)S(1)}, f32[768]{0:T(1024)S(1)}, /*index=5*/s32[]{:T(128)}, s32[]{:T(128)}) while((s32[]{:T(128)}, f32[16,512]{1,0:T(8,128)S(1)}, bf16[16,256,512]{2,1,0:T(8,128)(2,1)}, bf16[768,256]{1,0:T(8,128)(2,1)S(1)}, ...), condition=%wide.region_12.13_spmd, body=%wide.region_10.12_spmd.sunk | while | flops 202505728 | bytes 664669 | solution.py:72
  215.2 1.5 multiply_reduce_fusion.14
  220.0 1.5 multiply_reduce_fusion.14
  224.7 1.5 multiply_reduce_fusion.14
  229.5 1.5 multiply_reduce_fusion.14
  234.3 1.5 multiply_reduce_fusion.14
  237.5 69.5 %psum.65 = f32[8192]{0:T(1024)S(1)} all-reduce(f32[8192]{0:T(1024)S(1)} %bitcast.114), channel_id=1, replica_groups=mesh['row'=16,'proto'=8] {'row'}, use_global_device_ids=true, to_apply=%region_13.14 | all-reduce | flops 8192 | bytes 65536 | tf_op jit(solution)/shard_map/psum | solution.py:72
  307.1 24.7 %while.83 = (s32[]{:T(128)}, f32[768]{0:T(1024)S(1)}, bf16[16,256,512]{2,1,0:T(8,128)(2,1)}, bf16[768,256]{1,0:T(8,128)(2,1)S(1)}, f32[16,512]{1,0:T(8,128)S(1)}, /*index=5*/s32[]{:T(128)}, s32[]{:T(128)}) while((s32[]{:T(128)}, f32[768]{0:T(1024)S(1)}, bf16[16,256,512]{2,1,0:T(8,128)(2,1)}, bf16[768,256]{1,0:T(8,128)(2,1)S(1)}, ...), condition=%wide.region_16.17_spmd.clone, body=%wide.region_14.16_spmd.clone.sunk | while | flops 202507008 | bytes 673895 | solution.py:55
  331.7 12.4 %psum.66 = f32[768]{0:T(1024)S(1)} all-reduce(f32[768]{0:T(1024)S(1)} %get-tuple-element.227), channel_id=1, replica_groups=mesh['row'=16,'proto'=8] {'proto'}, use_global_device_ids=true, to_apply=%region_17.18 | all-reduce | flops 768 | bytes 6144 | tf_op jit(solution)/shard_map/psum | solution.py:74
  344.2 25.5 %while.80 = (s32[]{:T(128)}, f32[16,512]{1,0:T(8,128)S(1)}, bf16[16,256,512]{2,1,0:T(8,128)(2,1)}, bf16[768,256]{1,0:T(8,128)(2,1)S(1)}, f32[768]{0:T(1024)S(1)}, /*index=5*/s32[]{:T(128)}, s32[]{:T(128)}) while((s32[]{:T(128)}, f32[16,512]{1,0:T(8,128)S(1)}, bf16[16,256,512]{2,1,0:T(8,128)(2,1)}, bf16[768,256]{1,0:T(8,128)(2,1)S(1)}, ...), condition=%wide.region_20.21_spmd, body=%wide.region_18.20_spmd.sunk | while | flops 202505728 | bytes 664669 | solution.py:72
  347.4 1.5 multiply_reduce_fusion.15
  369.7 69.5 %psum.67 = f32[8192]{0:T(1024)S(1)} all-reduce(f32[8192]{0:T(1024)S(1)} %bitcast.115), channel_id=1, replica_groups=mesh['row'=16,'proto'=8] {'row'}, use_global_device_ids=true, to_apply=%region_21.22 | all-reduce | flops 8192 | bytes 65536 | tf_op jit(solution)/shard_map/psum | solution.py:72
  439.2 22.2 %while.84 = (s32[]{:T(128)}, f32[256]{0:T(256)S(1)}, f32[256]{0:T(256)S(1)}, bf16[16,256,512]{2,1,0:T(8,128)(2,1)}, bf16[256,256]{1,0:T(8,128)(2,1)S(1)}, /*index=5*/f32[16,512]{1,0:T(8,128)S(1)}, s32[]{:T(128)}, s32[]{:T(128)}) while((s32[]{:T(128)}, f32[256]{0:T(256)S(1)}, f32[256]{0:T(256)S(1)}, ...), condition=%wide.region_25.26_spmd.clone, body=%wide.region_22.25_spmd.clone.sunk | while | flops 67764736 | bytes 407663 | solution.py:93
  461.4 12.4 %all-reduce.1 = (f32[256]{0:T(256)S(1)}, f32[256]{0:T(256)S(1)}) all-reduce(f32[256]{0:T(256)S(1)} %get-tuple-element.229, f32[256]{0:T(256)S(1)} %get-tuple-element.230), channel_id=1, replica_groups=mesh['row'=16,'proto'=8] {'proto'}, use_global_device_ids=true, to_apply=%region_26.27 | all-reduce | flops 512 | bytes 4096 | tf_op jit(solution)/shard_map/psum | solution.py:96
  473.8 76.1 %while.81 = (s32[]{:T(128)}, f32[]{:T(128)}, bf16[16,256,512]{1,2,0:T(8,128)(2,1)}, bf16[16,256,512]{2,1,0:T(8,128)(2,1)}, bf16[256,256]{1,0:T(8,128)(2,1)S(1)},...) while((s32[]{:T(128)}, f32[]{:T(128)}, ...), condition=%wide.region_30.31_spmd.clone, body=%wide.region_28.30_spmd.clone.sunk | while | flops 170049536 | bytes 3946641 | solution.py:120
  550.0 5.5 fusion.45
  555.5 6.7 fusion.46
  562.3 62.9 %psum.71 = f32[]{:T(128)} all-reduce(f32[]{:T(128)} %get-tuple-element.232), channel_id=1, replica_groups=mesh['row'=16,'proto'=8] {'row','proto'}, use_global_device_ids=true, to_apply=%region_34.35 | all-reduce | flops 1 | bytes 8 | tf_op jit(solution)/shard_map/psum | solution.py:134
  627.0 1.8 fusion.41
  628.8 69.7 %reduce-scatter.2.cloned.1.call-done = f32[16,8192]{1,0:T(8,128)} async-done(((f32[256,8192]{1,0:T(8,128)}), f32[16,8192]{1,0:T(8,128)}) %reduce-scatter.2.cloned.1.call-update) | async-done | bytes 524304 | tf_op jit(solution)/shard_map/reduce_scatter | solution.py:126
  (349 shorter events, 200.9 us)
Async XLA Ops:
  7.2 57.0 %all-gather.2.cloned.1.call-start = ((), (), s32[]{:S(2)}) async-start(), calls=%async_computation.1 | async-start | bytes 4456448 | tf_op jit(solution)/shard_map/all_gather | solution.py:29
  7.9 617.9 %all-reduce.4.cloned.1.call-start = ((), (), s32[]{:S(2)}) async-start(), calls=%async_computation.2 | async-start | bytes 524288 | tf_op jit(solution)/shard_map/psum | solution.py:125
  555.5 143.1 %reduce-scatter.2.cloned.1.call-start = ((), (), s32[]{:S(2)}) async-start(), calls=%async_computation.3 | async-start | bytes 8912896 | tf_op jit(solution)/shard_map/reduce_scatter | solution.py:126
  562.2 63.6 %copy-start = (bf16[256,256]{1,0:T(8,128)(2,1)S(1)}, bf16[256,256]{1,0:T(8,128)(2,1)}, u32[]{:S(2)}) copy-start(bf16[256,256]{1,0:T(8,128)(2,1)} %param.19) | copy-start | bytes 393220
Sparse Core Ops, SparseCore 0:
  10.1 53.9 all-gather.1
  555.6 53.6 all-reduce.3
  613.2 85.2 reduce-scatter.1
where the time goes:
time: 711 us; the launch traced here: 706 us
  blocking collectives  312 us (44%)
  matrix products  205 us (29%)
  waiting for transfers between devices  121 us (17%)
  other arithmetic  21.7 us (3%)
  local copies, waits for them, and re-layouts  16.4 us (2%)
  between operations  16.4 us (2%)
  loops' own time  13.6 us (2%)
    psum x3, blocking collectives, body(): lax.psum(lax.map(column_block, blocks).reshape(width_local), 'row')  212 us
    dot_general x48, matrix products, column_block(): jnp.dot(rows_all, proto_block, preferred_element_type=jnp.float32)  72.5 us
    reduce_scatter x1, waiting for transfers between devices, body(): lax.psum_scatter(lax.dot_general(normed, logit_gradient, (((0,), (0,)), (...  69.7 us
    psum x1, blocking collectives, body(): loss_total = lax.psum(loss_local, ('row', 'proto'))  62.9 us
    all_gather x1, waiting for transfers between devices, body(): gathered = lax.all_gather(prototypes, 'row', axis=0, tiled=True)  50.5 us
    dot_general x32, matrix products, row_block(): jnp.dot(rows_all, proto_block, preferred_element_type=jnp.float32)  47.4 us
    psum x2, blocking collectives, body(): centroid_matrix = live / lax.psum(row_pass(column), 'proto')  24.9 us
    dot_general x16, matrix products, totals(): jnp.dot(normed, proto_block, preferred_element_type=jnp.float32)  21.2 us
  transfers between devices with their start and end apart: 3, of which 2 were waited for; matrix products, arithmetic and copies ran while one was open for 2% of the time, Pallas kernels for 0%

commit v1 on v0

--- a/solution.py
+++ b/solution.py
@@ -26,7 +26,9 @@
     local_image = crop_image - lax.axis_index("row") * image_local
     image_ids = jnp.arange(image_local, dtype=jnp.int32)
     membership = (image_ids[:, None] == local_image[None, :]).astype(jnp.bfloat16)
-    gathered = lax.all_gather(prototypes, "row", axis=0, tiled=True)
+    gathered = jnp.concatenate(
+        lax.all_to_all(jnp.stack([prototypes] * lax.axis_size("row")), "row", 0, 0), axis=0
+    )
     width_local = gathered.shape[1]
     block_cols = min(512, width_local)
     block_count = width_local // block_cols

time: 711 us -> 665 us (0.935)
  waiting for transfers between devices: 121 us -> 73.8 us
  starting transfers between devices: 0.12 us -> 8.43 us
    all_to_all x0 -> x1, waiting for transfers between devices: none -> 61.9 us  [body(): lax.all_to_all(jnp.stack([prototypes] * lax.axis_size('row')), 'row', 0, 0)]
    reduce_scatter x1, waiting for transfers between devices: 69.7 us -> 11.8 us  [body(): lax.psum_scatter(lax.dot_general(normed, logit_gradient, (((0,), (0,)), (...]
    all_gather x1 -> x0, waiting for transfers between devices: 50.5 us -> none  [body(): gathered = lax.all_gather(prototypes, 'row', axis=0, tiled=True)]
    all_to_all x0 -> x1, starting transfers between devices: none -> 8.34 us  [body(): lax.all_to_all(jnp.stack([prototypes] * lax.axis_size('row')), 'row', 0, 0)]
where the time goes in v1:
time: 665 us; the launch traced here: 661 us
  blocking collectives  312 us (47%)
  matrix products  202 us (30%)
  waiting for transfers between devices  73.8 us (11%)
  between operations  18.2 us (3%)
  other arithmetic  17.3 us (3%)
  local copies, waits for them, and re-layouts  15.3 us (2%)
  loops' own time  13.6 us (2%)
  starting transfers between devices  8.43 us (1%)
    psum x3, blocking collectives, body(): lax.psum(lax.map(column_block, blocks).reshape(width_local), 'row')  211 us
    dot_general x48, matrix products, column_block(): jnp.dot(rows_all, proto_block, preferred_element_type=jnp.float32)  72.5 us
    psum x1, blocking collectives, body(): loss_total = lax.psum(loss_local, ('row', 'proto'))  64.2 us
    all_to_all x1, waiting for transfers between devices, body(): lax.all_to_all(jnp.stack([prototypes] * lax.axis_size('row')), 'row', 0, 0)  61.9 us
    dot_general x32, matrix products, row_block(): jnp.dot(rows_all, proto_block, preferred_element_type=jnp.float32)  47.4 us
    psum x2, blocking collectives, body(): centroid_matrix = live / lax.psum(row_pass(column), 'proto')  24.9 us
    dot_general x16, matrix products, totals(): jnp.dot(normed, proto_block, preferred_element_type=jnp.float32)  21.2 us
    dot_general x16, matrix products, slopes(): lax.dot_general(member_weights, per_image, (((0,), (0,)), ((), ())), prec...  19.5 us
  transfers between devices with their start and end apart: 3, of which 2 were waited for; matrix products, arithmetic and copies ran while one was open for 2% of the time, Pallas kernels for 0%

profile of v1, /device:TPU:0, one launch (start us, length us, event | category | flops | bytes accessed | tf_op | source)
XLA Modules:
  0.0 661.1 jit_solution(15858840810303205915)
XLA Ops:
  8.0 3.4 stack.2
  11.4 8.3 %all-to-all-start = ((bf16[16,16,8192]{2,1,0:T(8,128)(2,1)}), bf16[16,16,8192]{2,1,0:T(8,128)(2,1)}, u32[]{:S(2)}, u32[]{:S(2)}) async-start(bf16[16,16,8192]{2,1,0:T(8,128)(2,1)} %stack.2), calls=%async_computation | async-start | bytes 8388608 | tf_op jit(solution)/shard_map/all_to_all | solution.py:30
  21.1 61.9 %all-to-all-done = bf16[16,16,8192]{2,1,0:T(8,128)(2,1)} async-done(((bf16[16,16,8192]{2,1,0:T(8,128)(2,1)}), bf16[16,16,8192]{2,1,0:T(8,128)(2,1)}, u32[]{:S(2)}, u32[]{:S(2)}) %all-to-all-start) | async-done | bytes 4194336 | tf_op jit(solution)/shard_map/all_to_all | solution.py:30
  83.0 4.0 copy.15
  87.1 4.4 copy.14
  91.4 25.4 %while.78 = (s32[]{:T(128)}, f32[16,512]{1,0:T(8,128)S(1)}, bf16[16,256,512]{2,1,0:T(8,128)(2,1)}, bf16[768,256]{1,0:T(8,128)(2,1)S(1)}, f32[768]{0:T(1024)S(1)}, /*index=5*/s32[]{:T(128)}, s32[]{:T(128)}) while((s32[]{:T(128)}, f32[16,512]{1,0:T(8,128)S(1)}, bf16[16,256,512]{2,1,0:T(8,128)(2,1)}, bf16[768,256]{1,0:T(8,128)(2,1)S(1)}, ...), condition=%wide.region_4.5_spmd, body=%wide.region_2.4_spmd.sunk | while | flops 202505728 | bytes 664669 | solution.py:74
  93.0 1.5 multiply_reduce_fusion.13
  116.9 71.6 %psum.63 = f32[8192]{0:T(1024)S(1)} all-reduce(f32[8192]{0:T(1024)S(1)} %bitcast.116), channel_id=1, replica_groups=mesh['row'=16,'proto'=8] {'row'}, use_global_device_ids=true, to_apply=%region_5.6 | all-reduce | flops 8192 | bytes 65536 | tf_op jit(solution)/shard_map/psum | solution.py:74
  188.5 24.6 %while.82 = (s32[]{:T(128)}, f32[768]{0:T(1024)S(1)}, bf16[16,256,512]{2,1,0:T(8,128)(2,1)}, bf16[768,256]{1,0:T(8,128)(2,1)S(1)}, f32[16,512]{1,0:T(8,128)S(1)}, /*index=5*/s32[]{:T(128)}, s32[]{:T(128)}) while((s32[]{:T(128)}, f32[768]{0:T(1024)S(1)}, bf16[16,256,512]{2,1,0:T(8,128)(2,1)}, bf16[768,256]{1,0:T(8,128)(2,1)S(1)}, ...), condition=%wide.region_8.9_spmd.clone, body=%wide.region_6.8_spmd.clone.sunk | while | flops 202507008 | bytes 673895 | solution.py:57
  213.1 12.4 %psum.64 = f32[768]{0:T(1024)S(1)} all-reduce(f32[768]{0:T(1024)S(1)} %get-tuple-element.225), channel_id=1, replica_groups=mesh['row'=16,'proto'=8] {'proto'}, use_global_device_ids=true, to_apply=%region_9.10 | all-reduce | flops 768 | bytes 6144 | tf_op jit(solution)/shard_map/psum | solution.py:76
  225.5 25.5 %while.79 = (s32[]{:T(128)}, f32[16,512]{1,0:T(8,128)S(1)}, bf16[16,256,512]{2,1,0:T(8,128)(2,1)}, bf16[768,256]{1,0:T(8,128)(2,1)S(1)}, f32[768]{0:T(1024)S(1)}, /*index=5*/s32[]{:T(128)}, s32[]{:T(128)}) while((s32[]{:T(128)}, f32[16,512]{1,0:T(8,128)S(1)}, bf16[16,256,512]{2,1,0:T(8,128)(2,1)}, bf16[768,256]{1,0:T(8,128)(2,1)S(1)}, ...), condition=%wide.region_12.13_spmd, body=%wide.region_10.12_spmd.sunk | while | flops 202505728 | bytes 664669 | solution.py:74
  225.6 1.5 multiply_reduce_fusion.14
  227.2 1.5 multiply_reduce_fusion.14
  228.7 1.5 multiply_reduce_fusion.14
  251.0 69.5 %psum.65 = f32[8192]{0:T(1024)S(1)} all-reduce(f32[8192]{0:T(1024)S(1)} %bitcast.117), channel_id=1, replica_groups=mesh['row'=16,'proto'=8] {'row'}, use_global_device_ids=true, to_apply=%region_13.14 | all-reduce | flops 8192 | bytes 65536 | tf_op jit(solution)/shard_map/psum | solution.py:74
  320.6 24.7 %while.83 = (s32[]{:T(128)}, f32[768]{0:T(1024)S(1)}, bf16[16,256,512]{2,1,0:T(8,128)(2,1)}, bf16[768,256]{1,0:T(8,128)(2,1)S(1)}, f32[16,512]{1,0:T(8,128)S(1)}, /*index=5*/s32[]{:T(128)}, s32[]{:T(128)}) while((s32[]{:T(128)}, f32[768]{0:T(1024)S(1)}, bf16[16,256,512]{2,1,0:T(8,128)(2,1)}, bf16[768,256]{1,0:T(8,128)(2,1)S(1)}, ...), condition=%wide.region_16.17_spmd.clone, body=%wide.region_14.16_spmd.clone.sunk | while | flops 202507008 | bytes 673895 | solution.py:57
  345.3 12.4 %psum.66 = f32[768]{0:T(1024)S(1)} all-reduce(f32[768]{0:T(1024)S(1)} %get-tuple-element.227), channel_id=1, replica_groups=mesh['row'=16,'proto'=8] {'proto'}, use_global_device_ids=true, to_apply=%region_17.18 | all-reduce | flops 768 | bytes 6144 | tf_op jit(solution)/shard_map/psum | solution.py:76
  357.7 25.5 %while.80 = (s32[]{:T(128)}, f32[16,512]{1,0:T(8,128)S(1)}, bf16[16,256,512]{2,1,0:T(8,128)(2,1)}, bf16[768,256]{1,0:T(8,128)(2,1)S(1)}, f32[768]{0:T(1024)S(1)}, /*index=5*/s32[]{:T(128)}, s32[]{:T(128)}) while((s32[]{:T(128)}, f32[16,512]{1,0:T(8,128)S(1)}, bf16[16,256,512]{2,1,0:T(8,128)(2,1)}, bf16[768,256]{1,0:T(8,128)(2,1)S(1)}, ...), condition=%wide.region_20.21_spmd, body=%wide.region_18.20_spmd.sunk | while | flops 202505728 | bytes 664669 | solution.py:74
  360.9 1.5 multiply_reduce_fusion.15
  365.7 1.5 multiply_reduce_fusion.15
  370.5 1.5 multiply_reduce_fusion.15
  375.2 1.5 multiply_reduce_fusion.15
  380.0 1.5 multiply_reduce_fusion.15
  383.2 69.5 %psum.67 = f32[8192]{0:T(1024)S(1)} all-reduce(f32[8192]{0:T(1024)S(1)} %bitcast.118), channel_id=1, replica_groups=mesh['row'=16,'proto'=8] {'row'}, use_global_device_ids=true, to_apply=%region_21.22 | all-reduce | flops 8192 | bytes 65536 | tf_op jit(solution)/shard_map/psum | solution.py:74
  452.8 22.2 %while.84 = (s32[]{:T(128)}, f32[256]{0:T(256)S(1)}, f32[256]{0:T(256)S(1)}, bf16[16,256,512]{2,1,0:T(8,128)(2,1)}, bf16[256,256]{1,0:T(8,128)(2,1)S(1)}, /*index=5*/f32[16,512]{1,0:T(8,128)S(1)}, s32[]{:T(128)}, s32[]{:T(128)}) while((s32[]{:T(128)}, f32[256]{0:T(256)S(1)}, f32[256]{0:T(256)S(1)}, ...), condition=%wide.region_25.26_spmd.clone, body=%wide.region_22.25_spmd.clone.sunk | while | flops 67764736 | bytes 407663 | solution.py:95
  474.9 12.6 %all-reduce.1 = (f32[256]{0:T(256)S(1)}, f32[256]{0:T(256)S(1)}) all-reduce(f32[256]{0:T(256)S(1)} %get-tuple-element.229, f32[256]{0:T(256)S(1)} %get-tuple-element.230), channel_id=1, replica_groups=mesh['row'=16,'proto'=8] {'proto'}, use_global_device_ids=true, to_apply=%region_26.27 | all-reduce | flops 512 | bytes 4096 | tf_op jit(solution)/shard_map/psum | solution.py:98
  487.6 73.1 %while.81 = (s32[]{:T(128)}, f32[]{:T(128)}, bf16[16,256,512]{1,2,0:T(8,128)(2,1)}, bf16[16,256,512]{2,1,0:T(8,128)(2,1)}, bf16[256,256]{1,0:T(8,128)(2,1)S(1)},...) while((s32[]{:T(128)}, f32[]{:T(128)}, ...), condition=%wide.region_30.31_spmd.clone, body=%wide.region_28.30_spmd.clone.sunk | while | flops 170049536 | bytes 3946641 | solution.py:122
  560.6 5.5 fusion.45
  566.2 6.7 %fusion.46 = f32[256,8192]{1,0:T(8,128)} fusion(bf16[256,256]{1,0:T(8,128)(2,1)S(1)} %get-tuple-element.878, bf16[256,8192]{0,1:T(8,128)(2,1)} %bitcast.112), kind=kOutput, calls=%fused_computation.77 | convolution fusion | flops 1073741824 | bytes 12713984 | tf_op jit(solution)/shard_map/dot_general | solution.py:129
  572.9 64.2 %psum.71 = f32[]{:T(128)} all-reduce(f32[]{:T(128)} %get-tuple-element.232), channel_id=1, replica_groups=mesh['row'=16,'proto'=8] {'row','proto'}, use_global_device_ids=true, to_apply=%region_34.35 | all-reduce | flops 1 | bytes 8 | tf_op jit(solution)/shard_map/psum | solution.py:136
  638.9 1.8 fusion.41
  640.7 11.8 %reduce-scatter.2.cloned.1.call-done = f32[16,8192]{1,0:T(8,128)} async-done(((f32[256,8192]{1,0:T(8,128)}), f32[16,8192]{1,0:T(8,128)}) %reduce-scatter.2.cloned.1.call-update) | async-done | bytes 524304 | tf_op jit(solution)/shard_map/reduce_scatter | solution.py:128
  (353 shorter events, 195.7 us)
Async XLA Ops:
  11.4 9.1 %copy-start = (bf16[256,256]{1,0:T(8,128)(2,1)S(1)}, bf16[256,256]{1,0:T(8,128)(2,1)}, u32[]{:S(2)}) copy-start(bf16[256,256]{1,0:T(8,128)(2,1)} %param.19) | copy-start | bytes 393220
  11.4 9.3 %copy-start.1 = (bf16[512,256]{1,0:T(8,128)(2,1)S(1)}, bf16[512,256]{1,0:T(8,128)(2,1)}, u32[]{:S(2)}) copy-start(bf16[512,256]{1,0:T(8,128)(2,1)} %param.20) | copy-start | bytes 786436
  11.4 9.7 %copy-start.2 = (s32[256]{0:T(256)S(1)}, s32[256]{0:T(256)}, u32[]{:S(2)}) copy-start(s32[256]{0:T(256)} %param.22) | copy-start | bytes 3076
  11.4 71.6 %all-to-all-start = ((bf16[16,16,8192]{2,1,0:T(8,128)(2,1)}), bf16[16,16,8192]{2,1,0:T(8,128)(2,1)}, u32[]{:S(2)}, u32[]{:S(2)}) async-start(bf16[16,16,8192]{2,1,0:T(8,128)(2,1)} %stack.2), calls=%async_computation | async-start | bytes 8388608 | tf_op jit(solution)/shard_map/all_to_all | solution.py:30
  19.7 618.1 %all-reduce.4.cloned.1.call-start = ((), (), s32[]{:S(2)}) async-start(), calls=%async_computation.2 | async-start | bytes 524288 | tf_op jit(solution)/shard_map/psum | solution.py:127
  566.1 86.5 %reduce-scatter.2.cloned.1.call-start = ((), (), s32[]{:S(2)}) async-start(), calls=%async_computation.3 | async-start | bytes 8912896 | tf_op jit(solution)/shard_map/reduce_scatter | solution.py:128
Sparse Core Ops, SparseCore 0:
  566.2 54.1 all-reduce.3
Sparse Core Ops, SparseCore 1:
  573.0 79.5 reduce-scatter.1
